TPU v7x, 512 devices: a whole 4x8x8 slice. The times are simulated.
512 devices in a mesh: left: 4 (over y_lo, core), right: 16 (over x, y_hi), occ: 8 (over z).
Axes of the slice: x: 4, y: 8 (y_hi: 4, y_lo: 2; y = y_hi * 2 + y_lo), z: 8, core: 2. Of those that a mesh axis runs over, the one named last changes fastest.
Arguments:
- chol: bfloat16 [16, 1024, 2048], P('right', 'occ', 'left'), may hold values from -0.125 to 0.125
- amps: bfloat16 [4, 4, 1024, 512], P('left', None, 'occ', 'right'), may hold values from -1.5 to 1.5
- listed: int32 [4, 4, 4, 4], replicated, may hold values 0 or 1
Outputs:
- residual: float32 [4, 4, 1024, 512], P('left', None, 'occ', 'right')
All inputs are finite; a program needn't handle non-finite values.
Results may differ from a plain program's by a relative error of at most 0.0029.
Values may be sent and summed in bfloat16 or wider, within the bound.
A program may use at most 64 MiB of HBM per device.

v0:
```python
import jax
import jax.numpy as jnp
from jax import lax
from jax.sharding import PartitionSpec as P

TV = 32
NTV = 4
NQ = 2048
NOP = 512
PAIR = 1024


def on_device(chol, amps, listed):
    tile_count = chol.shape[0]
    row_count = chol.shape[1]
    a_local = row_count // TV
    left_index = lax.axis_index("left")
    right_index = lax.axis_index("right")
    first_tile = right_index * tile_count
    full_vectors = lax.all_gather(chol, "left", axis=2, tiled=True)
    every_tile = lax.all_gather(full_vectors, "right", axis=0, tiled=True)
    every_tile = every_tile.reshape(NTV, NTV, row_count, NQ)
    left_rows = lax.dynamic_index_in_dim(every_tile, left_index, 1, keepdims=False)
    own_c = lax.dynamic_index_in_dim(listed, left_index, 1, keepdims=False).reshape(NTV, NTV * NTV)
    live = lax.dynamic_slice_in_dim(own_c, first_tile, tile_count, 1).T.astype(jnp.float32)
    products = jnp.einsum(
        "xrq,tkq->txrk",
        left_rows,
        lax.all_gather(full_vectors, "occ", axis=1, tiled=True),
        preferred_element_type=jnp.float32,
    )
    inner = (products * live[:, :, None, None]).astype(jnp.bfloat16)
    swapped = inner.reshape(tile_count, NTV, a_local, TV, TV, TV).transpose(0, 1, 2, 4, 3, 5)
    swapped = swapped.reshape(tile_count, NTV * a_local * TV, PAIR)
    amp_columns = lax.all_gather(amps, "right", axis=3, tiled=True)
    d_first = first_tile % NTV
    own_amps = lax.dynamic_slice_in_dim(amp_columns[0], d_first, tile_count, 0)
    partial_sum = jnp.einsum(
        "trk,tkn->rn",
        swapped,
        lax.all_gather(own_amps, "occ", axis=1, tiled=True),
        preferred_element_type=jnp.float32,
    )
    partial_sum = partial_sum.reshape(NTV, row_count, NOP)
    owned_a = lax.psum_scatter(partial_sum, "left", scatter_dimension=0, tiled=True)
    b_tile = first_tile // NTV
    placed = lax.dynamic_update_slice_in_dim(
        jnp.zeros((NTV, row_count, NOP), jnp.float32), owned_a, b_tile, 0
    )
    summed = lax.psum_scatter(placed, "right", scatter_dimension=2, tiled=True)
    return summed.reshape(1, NTV, row_count, summed.shape[2])


def solution(mesh):
    placed = (P("right", "occ", "left"), P("left", None, "occ", "right"), P())
    return jax.shard_map(
        on_device,
        mesh=mesh,
        in_specs=placed,
        out_specs=P("left", None, "occ", "right"),
        check_vma=False,
    )
```

profile of v0, /device:TPU:1, one launch (start us, length us, event | category | flops | bytes accessed | tf_op | source)
XLA Modules:
  0.0 373.2 jit_solution(13207223785238778920)
XLA Ops:
  6.5 0.0 copy-start
  6.5 0.0 all-gather.7.cloned.1.call-start
  6.5 14.0 %all_gather.15 = bf16[1,128,2048]{2,1,0:T(8,128)(2,1)} all-gather(bf16[1,128,512]{2,1,0:T(8,128)(2,1)} %param.3), channel_id=1, replica_groups=mesh['left'=4,'right'=16,'occ'=8] {'left'}, dimensions={2}, use_global_device_ids=true | all-gather | bytes 655360 | tf_op jit(solution)/shard_map/all_gather | solution.py:20
  20.5 0.0 all-gather.7.cloned.1.call-update
  20.5 0.0 all-gather.5.cloned.1.call-start
  20.6 0.7 all-gather.5.cloned.1.call-update
  21.3 0.0 all-gather.9.cloned.1.call-start
  21.3 0.8 copy.12
  22.1 36.3 %all_gather.18 = bf16[1,4,128,512]{2,1,0,3:T(4,128)(2,1)S(1)} all-gather(bf16[1,4,128,32]{2,1,0,3:T(4,128)(2,1)S(1)} %copy.12), channel_id=1, replica_groups=mesh['left'=4,'right'=16,'occ'=8] {'right'}, dimensions={3}, use_global_device_ids=true | all-gather | bytes 557056 | tf_op jit(solution)/shard_map/all_gather | solution.py:35
  58.4 0.3 constant_dynamic-slice_fusion
  58.7 0.8 copy.16
  59.5 0.0 all-gather.9.cloned.1.call-update
  59.5 0.0 reduce-scatter.3.cloned.1.call-start
  59.6 0.0 copy-done
  59.6 0.1 reshape.40
  59.7 0.2 convert_reduce_fusion
  59.9 18.4 %all-gather.7.cloned.1.call-done = bf16[1,1024,2048]{2,1,0:T(8,128)(2,1)} async-done(((bf16[1,128,2048]{2,1,0:T(8,128)(2,1)}), bf16[1,1024,2048]{2,1,0:T(8,128)(2,1)}) %all-gather.7.cloned.1.call-update) | async-done | bytes 4194320 | tf_op jit(solution)/shard_map/all_gather | solution.py:29
  78.3 122.5 %all-gather.5.cloned.1.call-done = bf16[16,128,2048]{2,1,0:T(8,128)(2,1)} async-done(((bf16[1,128,2048]{2,1,0:T(8,128)(2,1)}), bf16[16,128,2048]{2,1,0:T(8,128)(2,1)}) %all-gather.5.cloned.1.call-update) | async-done | bytes 8388624 | tf_op jit(solution)/shard_map/all_gather | solution.py:21
  200.8 5.2 %fusion.9 = bf16[1,4,128,1024]{3,2,1,0:T(8,128)(2,1)S(1)} fusion(bf16[1,1024,2048]{2,1,0:T(8,128)(2,1)} %all-gather.7.cloned.1.call-done, bf16[4,4,128,2048]{3,2,1,0:T(8,128)(2,1)} %bitcast.41, s32[]{:T(128)S(6)} %select_n.26, f32[4]{0:T(128)S(1)} %convert_reduce_fusion), kind=kOutput, calls=%fused_computation.6 | convolution fusion | flops 2148532224 | bytes 7340052 | tf_op jit(solution)/shard_map/xrq,tkq->txrk/dot_general | solution.py:26
  206.0 4.4 %reshape.41 = bf16[1,4,4,32,32,32]{5,4,3,2,1,0:T(8,128)(2,1)} reshape(bf16[1,4,128,1024]{3,2,1,0:T(8,128)(2,1)S(1)} %fusion.9) | data formatting | bytes 2097152 | tf_op jit(solution)/shard_map/reshape | solution.py:33
  210.4 5.9 %copy.11 = bf16[1,4,4,32,32,32]{5,4,3,2,1,0:T(8,128)(2,1)} copy(bf16[1,4,4,32,32,32]{5,3,4,2,1,0:T(8,128)(2,1)} %bitcast.40) | data formatting | bytes 2097152 | tf_op jit(solution)/shard_map/transpose | solution.py:33
  216.3 6.2 %dot_general.15 = bf16[4,128,1024]{2,1,0:T(8,128)(2,1)S(1)} reshape(bf16[1,4,4,32,32,32]{5,4,3,2,1,0:T(8,128)(2,1)} %copy.11) | data formatting | bytes 2097152 | tf_op jit(solution)/shard_map/trk,tkn->rn/dot_general | solution.py:38
  222.5 17.3 %all-gather.9.cloned.1.call-done = bf16[1,1,1024,512]{3,2,1,0:T(8,128)(2,1)} async-done(((bf16[1,1,128,512]{3,2,1,0:T(8,128)(2,1)}), bf16[1,1,1024,512]{3,2,1,0:T(8,128)(2,1)}) %all-gather.9.cloned.1.call-update) | async-done | bytes 1048592 | tf_op jit(solution)/shard_map/all_gather | solution.py:41
  239.8 2.9 fusion.14
  242.7 0.0 reduce-scatter.3.cloned.1.call-update
  242.7 0.0 reduce-scatter.5.cloned.1.call-start
  242.8 28.9 %reduce-scatter.3.cloned.1.call-done = f32[1,128,512]{2,1,0:T(8,128)} async-done(((f32[4,128,512]{2,1,0:T(8,128)}), f32[1,128,512]{2,1,0:T(8,128)}) %reduce-scatter.3.cloned.1.call-update) | async-done | bytes 262160 | tf_op jit(solution)/shard_map/reduce_scatter | solution.py:45
  271.7 1.1 copy.14
  272.8 0.1 broadcast_in_dim.4
  272.9 0.0 copy-start.1
  272.9 1.0 copy-done.1
  273.8 0.0 reduce-scatter.5.cloned.1.call-update
  273.9 92.8 %reduce-scatter.5.cloned.1.call-done = f32[4,128,32]{1,2,0:T(8,128)} async-done(((f32[4,128,512]{1,2,0:T(8,128)}), f32[4,128,32]{1,2,0:T(8,128)}) %reduce-scatter.5.cloned.1.call-update) | async-done | bytes 65552 | tf_op jit(solution)/shard_map/reduce_scatter | solution.py:50
  (2 shorter events, 0.0 us)
Async XLA Ops:
  6.5 53.0 %copy-start = (s32[4,4,4,4]{3,2,1,0:T(4,128)S(1)}, s32[4,4,4,4]{3,2,1,0:T(4,128)}, u32[]{:S(2)}) copy-start(s32[4,4,4,4]{3,2,1,0:T(4,128)} %param.5) | copy-start | bytes 3076
  6.5 71.7 %all-gather.7.cloned.1.call-start = ((), (), s32[]{:S(2)}) async-start(), calls=%async_computation.3 | async-start | bytes 4718592 | tf_op jit(solution)/shard_map/all_gather | solution.py:29
  20.5 180.3 %all-gather.5.cloned.1.call-start = ((), (), s32[]{:S(2)}) async-start(), calls=%async_computation.2 | async-start | bytes 8912896 | tf_op jit(solution)/shard_map/all_gather | solution.py:21
  21.3 218.5 %all-gather.9.cloned.1.call-start = ((), (), s32[]{:S(2)}) async-start(), calls=%async_computation.6 | async-start | bytes 1179648 | tf_op jit(solution)/shard_map/all_gather | solution.py:41
  59.5 212.2 %reduce-scatter.3.cloned.1.call-start = ((), (), s32[]{:S(2)}) async-start(), calls=%async_computation.4 | async-start | bytes 1310720 | tf_op jit(solution)/shard_map/reduce_scatter | solution.py:45
  242.7 123.9 %reduce-scatter.5.cloned.1.call-start = ((), (), s32[]{:S(2)}) async-start(), calls=%async_computation.5 | async-start | bytes 1114112 | tf_op jit(solution)/shard_map/reduce_scatter | solution.py:50
  272.9 1.0 copy-start.1
Sparse Core Ops, SparseCore 0:
  20.6 57.5 all-gather.6
  81.3 119.4 all-gather.4
  202.9 36.8 all-gather.8
  242.8 28.8 reduce-scatter.2
  275.6 90.9 reduce-scatter.4
where the time goes:
time: 374 us; the launch traced here: 373 us
  waiting for transfers between devices  281 us (75%)
  blocking collectives  50.3 us (13%)
  local copies, waits for them, and re-layouts  20.5 us (5%)
  between operations  13.3 us (4%)
  matrix products  8.08 us (2%)
    all_gather x1, waiting for transfers between devices, on_device(): every_tile = lax.all_gather(full_vectors, 'right', axis=0, tiled=True)  123 us
    reduce_scatter x1, waiting for transfers between devices, on_device(): summed = lax.psum_scatter(placed, 'right', scatter_dimension=2, tiled=True)  92.8 us
    all_gather x1, blocking collectives, on_device(): amp_columns = lax.all_gather(amps, 'right', axis=3, tiled=True)  36.3 us
    reduce_scatter x1, waiting for transfers between devices, on_device(): lax.psum_scatter(partial_sum, 'left', scatter_dimension=0, tiled=True)  28.9 us
    all_gather x1, waiting for transfers between devices, on_device(): lax.all_gather(full_vectors, 'occ', axis=1, tiled=True)  18.4 us
    all_gather x1, waiting for transfers between devices, on_device(): lax.all_gather(own_amps, 'occ', axis=1, tiled=True)  17.3 us
    all_gather x1, blocking collectives, on_device(): full_vectors = lax.all_gather(chol, 'left', axis=2, tiled=True)  14 us
  transfers between devices with their start and end apart: 5, of which 5 were waited for; matrix products, arithmetic and copies ran while one was open for 6% of the time, Pallas kernels for 0%

commit v1 on v0

v1 whole, which is shorter than its diff:
```python
import jax
import jax.numpy as jnp
from jax import lax
from jax.experimental import pallas as pl
from jax.experimental.pallas import tpu as pltpu
from jax.sharding import PartitionSpec as P

NTV = 4
MESH = pl.DeviceIdType.MESH
NT = (((1,), (1,)), ((), ()))


def kernel(
    listed, chol, amps, out,
    bd, xb, pb, tb, v, w, rs, rr, rx, ob,
    bd_r, bdp_r, xb_r, pb_r, t1_r, t2_r, tx_r, tp_r, rr_r, ob_r,
    loc_s, y_s, z_s, x_s, bdp_s, pb_s, t1_s, t2_s, tx_s, tp_s, rr_s, ob_s,
):
    left = lax.axis_index("left")
    right = lax.axis_index("right")
    z = lax.axis_index("occ")
    yl, c = left // 2, left % 2
    x, yh = right // 4, right % 4
    y = 2 * yh + yl
    oc = 1 - c
    s = 1 - 2 * c
    xf, xk, xo = (x + s + 4) % 4, (x - s + 4) % 4, (x + 2) % 4
    zf, zk = (z + s + 8) % 8, (z - s + 8) % 8

    def dev(x_=x, y_=y, z_=z, c_=c):
        return (2 * (y_ % 2) + c_, 4 * x_ + y_ // 2, z_)

    def remote(src, dst, ssem, rsem, to):
        return pltpu.make_async_remote_copy(
            src_ref=src, dst_ref=dst, send_sem=ssem, recv_sem=rsem, device_id=to, device_id_type=MESH
        )

    partner = dev(c_=oc)

    barrier = pltpu.get_barrier_semaphore()

    def greet(to):
        pl.semaphore_signal(barrier, inc=1, device_id=to, device_id_type=MESH)

    greet(partner)
    for k in range(1, 8):
        greet(dev(y_=(y + k) % 8))
        greet(dev(z_=(z + k) % 8))
    for k in range(1, 4):
        greet(dev(x_=(x + k) % 4))
    pl.semaphore_wait(barrier, 18)

    def t1(k):
        d = (yh + k) % 4
        return remote(
            amps.at[d], tb.at[c, x, z, pl.ds(pl.multiple_of(yh * 32, 32), 32)], t1_s.at[k], t1_r,
            dev(y_=2 * d + yl),
        )

    t1_own = pltpu.make_async_copy(amps.at[yh], tb.at[c, x, z, pl.ds(pl.multiple_of(yh * 32, 32), 32)], t1_r)
    for k in range(1, 4):
        t1(k).start()
    t1_own.start()

    half, slot = y // 4, y % 4
    bd_own = pltpu.make_async_copy(chol, bd.at[yl, c, z], bd_r.at[yl, z])
    bd_own.start()
    to_pair = remote(chol, bd.at[yl, c, z], y_s.at[4], bd_r.at[yl, z], dev(y_=y + 1 - 2 * yl))
    to_pair.start()

    def z_send(u, t, forward):
        yq = (yl + u) % 2
        if forward:
            zz = (z - s * t + 8) % 8
            return remote(bd.at[yq, c, zz], bd.at[yq, c, zz], z_s.at[0, u, t], bd_r.at[yq, zz], dev(z_=zf))
        zz = (z + s * t + 8) % 8
        return remote(bd.at[yq, c, zz], bd.at[yq, c, zz], z_s.at[1, u, t], bd_r.at[yq, zz], dev(z_=zk))

    def bd_wait(u, zz):
        yq = (yl + u) % 2
        pltpu.make_async_copy(bd.at[yq, c, zz], bd.at[yq, c, zz], bd_r.at[yq, zz]).wait()

    def bd_share(u, zz):
        yq = (yl + u) % 2
        return remote(bd.at[yq, c, zz], bd.at[yq, c, zz], bdp_s.at[u, zz], bdp_r.at[yq, zz], partner)

    near = [2 * ((yh + k) % 4) + half for k in range(4)]
    for k in (0, 1, 3, 2):
        @pl.when(near[k] != y)
        def _(k=k):
            remote(chol, xb.at[x, slot], y_s.at[k], xb_r.at[x, slot], dev(y_=near[k])).start()

        @pl.when(near[k] == y)
        def _():
            pltpu.make_async_copy(chol, xb.at[x, slot], xb_r.at[x, slot]).start()

    bd_wait(0, z)
    z_send(0, 0, True).start()
    z_send(0, 0, False).start()
    bd_share(0, z).start()
    bd_wait(1, z)
    z_send(1, 0, True).start()
    z_send(1, 0, False).start()
    bd_share(1, z).start()

    pow4 = (1 + 3 * (y % 2)) * (1 + 15 * ((y // 2) % 2)) * (1 + 255 * (y // 4))
    pow2 = (1 + y % 2) * (1 + 3 * ((y // 2) % 2)) * (1 + 15 * (y // 4))
    firsts = sum(f * 4**i for i, f in enumerate((0, 3, 2, 0, 3, 1, 0, 3)))
    downs = sum(f * 2**i for i, f in enumerate((0, 1, 1, 0, 1, 0, 1, 1)))
    h0 = (firsts // pow4) % 4
    hs = 1 - 2 * ((downs // pow2) % 2)
    hs4 = [(h0 + hs * i + 4) % 4 for i in range(4)]

    def x_wait(a, h):
        pltpu.make_async_copy(xb.at[a, h], xb.at[a, h], xb_r.at[a, h]).wait()

    def x_send(a, i, to, which):
        h = hs4[i]
        return remote(xb.at[a, h], xb.at[a, h], x_s.at[which, i], xb_r.at[a, h], dev(x_=to))

    def x_share(a, h):
        return remote(xb.at[a, h], pb.at[a // 2, h], pb_s.at[a // 2, h], pb_r.at[a // 2, h], partner)

    def x_share_if(a, h):
        @pl.when(a % 2 != c)
        def _():
            x_share(a, h).start()

    def t2(k):
        return remote(tb.at[c, x, z], tb.at[c, x, z], t2_s.at[k], t2_r.at[z], dev(z_=(z + k) % 8))

    def tx(a, to, which):
        return remote(tb.at[c, a], tb.at[c, a], tx_s.at[which], tx_r.at[a], dev(x_=to))

    def tx_wait(a):
        pltpu.make_async_copy(tb.at[c, a], tb.at[c, a], tx_r.at[a]).wait()

    def t_share(a):
        return remote(tb.at[c, a], tb.at[c, a], tp_s.at[a], tp_r.at[a], partner)

    for j in range(8):
        if j < 4:
            x_wait(x, hs4[j])
            x_send(x, j, xf, 0).start()
            x_send(x, j, xk, 1).start()
            x_share_if(x, hs4[j])
        if j == 0:
            pltpu.make_async_copy(tb.at[c, x, z], tb.at[c, x, z], t1_r).wait()
            for k in (1, 7, 2, 6, 3, 5, 4):
                t2(k).start()
        u, t = j % 2, j // 2 + 1
        zz = (z - s * t + 8) % 8
        bd_wait(u, zz)
        if t < 4:
            z_send(u, t, True).start()
        bd_share(u, zz).start()
        if t < 4:
            zz = (z + s * t + 8) % 8
            bd_wait(u, zz)
            if t < 3:
                z_send(u, t, False).start()
            bd_share(u, zz).start()
        if j == 3:
            for k in range(1, 8):
                zk_ = (z + k) % 8
                pltpu.make_async_copy(tb.at[c, x, zk_], tb.at[c, x, zk_], t2_r.at[zk_]).wait()
            tx(x, xf, 0).start()
            tx(x, xk, 1).start()
            t_share(x).start()
        if 2 <= j < 6:
            h = hs4[j - 2]
            x_wait(xk, h)
            x_send(xk, j - 2, xf, 2).start()
            x_share_if(xk, h)
            x_wait(xf, h)
            x_share_if(xf, h)
        if j >= 4:
            h = hs4[j - 4]
            x_wait(xo, h)
            x_share_if(xo, h)
    tx_wait(xk)
    tx(xk, xf, 2).start()
    t_share(xk).start()
    tx_wait(xf)
    t_share(xf).start()

    for a in range(2):
        for h in range(4):
            pltpu.make_async_copy(pb.at[a, h], pb.at[a, h], pb_r.at[a, h]).wait()
    for q in range(2):
        for zz in range(8):
            pltpu.make_async_copy(bd.at[q, oc, zz], bd.at[q, oc, zz], bdp_r.at[q, zz]).wait()

    live = [
        [listed[((c + 2 * a) * NTV + 2 * yl + cc) * NTV * NTV + x * NTV + yh].astype(jnp.float32) for a in range(2)]
        for cc in range(2)
    ]

    def integrals(n, carry):
        total = None
        for q in range(2):
            rows = [xb[c + 2 * a, 2 * cc + q] for cc in range(2) for a in range(2)]
            cols = bd[q, c, pl.ds(2 * n, 2)].reshape(256, 512)
            part = lax.dot_general(jnp.concatenate(rows, 0), cols, NT, preferred_element_type=jnp.float32)
            total = part if total is None else total + part
            rows = [pb[a, 2 * cc + q] for cc in range(2) for a in range(2)]
            cols = bd[q, oc, pl.ds(2 * n, 2)].reshape(256, 512)
            total = total + lax.dot_general(
                jnp.concatenate(rows, 0), cols, NT, preferred_element_type=jnp.float32
            )
        for cc in range(2):
            for a in range(2):
                lo = (2 * cc + a) * 128
                block = total[lo : lo + 128] * live[cc][a]
                v[2 * n, pl.ds(lo, 128), :] = block[:, :128]
                v[2 * n + 1, pl.ds(lo, 128), :] = block[:, 128:]
        return carry

    lax.fori_loop(0, 4, integrals, 0)

    group = lax.broadcasted_iota(jnp.int32, (8, 128), 1) // 32
    odd, high = group % 2 == 1, group >= 2

    def swap(i, carry):
        cc, g = i // 8, i % 8
        for zz in range(8):
            r = [v[zz, pl.ds(cc * 256 + 4 * g + j, 8, stride=32), :] for j in range(4)]
            p = [None] * 4
            for j in (0, 2):
                p[j] = jnp.where(odd, pltpu.roll(r[j + 1], 32, 1), r[j])
                p[j + 1] = jnp.where(odd, r[j + 1], pltpu.roll(r[j], 96, 1))
            for j in (0, 1):
                w[i, pl.ds(4 * zz + j, 8, stride=32), :] = jnp.where(high, pltpu.roll(p[j + 2], 64, 1), p[j])
                w[i, pl.ds(4 * zz + j + 2, 8, stride=32), :] = jnp.where(high, p[j + 2], pltpu.roll(p[j], 64, 1))
        return carry

    lax.fori_loop(0, 16, swap, 0)

    tx_wait(xo)
    t_share(xo).start()
    for a in range(4):
        pltpu.make_async_copy(tb.at[oc, a], tb.at[oc, a], tp_r.at[a]).wait()

    def contract(n, carry):
        total = None
        for i in range(0, 16, 2):
            t = jnp.concatenate([tb[i // 8, n, i % 8], tb[i // 8, n, i % 8 + 1]], 1)
            m = jnp.concatenate([w[i].astype(jnp.bfloat16), w[i + 1].astype(jnp.bfloat16)], 1)
            part = lax.dot_general(t, m, NT, preferred_element_type=jnp.float32)
            total = part if total is None else total + part
        total = total.astype(jnp.bfloat16)
        for i in range(4):
            for a in range(2):
                rs[2 * i + a, n] = total[32 * i : 32 * i + 32, 128 * a : 128 * a + 128]
        return carry

    lax.fori_loop(0, 4, contract, 0)

    def r1(k):
        to = (y + k) % 8
        return remote(rs.at[to], rr.at[y], rr_s.at[k], rr_r.at[y], dev(y_=to))

    for k in (1, 7, 2, 6, 3, 5, 4):
        r1(k).start()
    total = rs[y].astype(jnp.float32)
    for k in (1, 7, 2, 6, 3, 5, 4):
        f = (y + k) % 8
        pltpu.make_async_copy(rr.at[f], rr.at[f], rr_r.at[f]).wait()
        total = total + rr[f].astype(jnp.float32)
    rx[...] = total

    def r2(k):
        to = (x + k) % 4
        return remote(rx.at[to], ob.at[x], ob_s.at[k], ob_r.at[x], dev(x_=to))

    for k in (1, 3, 2):
        r2(k).start()
    out[x] = rx[x]

    for k in range(1, 4):
        t1(k).wait_send()
        t2(k).wait_send()
        t2(k + 4).wait_send()
    t2(4).wait_send()
    to_pair.wait_send()
    for k in range(4):
        @pl.when(near[k] != y)
        def _(k=k):
            remote(chol, xb.at[x, slot], y_s.at[k], xb_r.at[x, slot], dev(y_=near[k])).wait_send()
    for u in range(2):
        for t in range(4):
            z_send(u, t, True).wait_send()
            if t < 3:
                z_send(u, t, False).wait_send()
        for zz in range(8):
            bd_share(u, zz).wait_send()
    for i in range(4):
        x_send(x, i, xf, 0).wait_send()
        x_send(x, i, xk, 1).wait_send()
        x_send(xk, i, xf, 2).wait_send()
        t_share(i).wait_send()
        for a in range(2):
            x_share(oc + 2 * a, i).wait_send()
    tx(x, xf, 0).wait_send()
    tx(x, xk, 1).wait_send()
    tx(xk, xf, 2).wait_send()
    for k in range(1, 8):
        r1(k).wait_send()
    for k in range(1, 4):
        r2(k).wait_send()
    for k in (1, 3, 2):
        f = (x + k) % 4
        pltpu.make_async_copy(ob.at[f], ob.at[f], ob_r.at[f]).wait()
        out[f] = ob[f]


def on_device(chol, amps, listed):
    bf16, f32, dma = jnp.bfloat16, jnp.float32, pltpu.SemaphoreType.DMA
    anyspace = pl.BlockSpec(memory_space=pl.ANY)
    out = pl.pallas_call(
        kernel,
        out_shape=jax.ShapeDtypeStruct((4, 32, 128), f32),
        in_specs=[pl.BlockSpec(memory_space=pltpu.SMEM), anyspace, anyspace],
        out_specs=pl.BlockSpec(memory_space=pltpu.VMEM),
        scratch_shapes=[
            pltpu.VMEM((2, 2, 8, 128, 512), bf16),
            pltpu.VMEM((4, 4, 128, 512), bf16),
            pltpu.VMEM((2, 4, 128, 512), bf16),
            pltpu.VMEM((2, 4, 8, 128, 128), bf16),
            pltpu.VMEM((8, 512, 128), f32),
            pltpu.VMEM((16, 256, 128), f32),
            pltpu.VMEM((8, 4, 32, 128), bf16),
            pltpu.VMEM((8, 4, 32, 128), bf16),
            pltpu.VMEM((4, 32, 128), f32),
            pltpu.VMEM((4, 32, 128), f32),
            dma((2, 8)), dma((2, 8)), dma((4, 4)), dma((2, 4)), dma, dma((8,)), dma((4,)), dma((4,)), dma((8,)), dma((4,)),
            dma, dma((5,)), dma((2, 2, 4)), dma((3, 4)), dma((2, 8)), dma((2, 4)), dma((4,)), dma((8,)), dma((3,)), dma((4,)), dma((8,)), dma((4,)),
        ],
        compiler_params=pltpu.CompilerParams(
            collective_id=0, has_side_effects=True, vmem_limit_bytes=60 * 1024 * 1024
        ),
    )(listed.reshape(-1), chol[0], jnp.swapaxes(amps[0], 1, 2))
    return jnp.swapaxes(out, 1, 2)[None]


def solution(mesh):
    placed = (P("right", "occ", "left"), P("left", None, "occ", "right"), P())
    return jax.shard_map(
        on_device,
        mesh=mesh,
        in_specs=placed,
        out_specs=P("left", None, "occ", "right"),
        check_vma=False,
    )
```

time: 374 us -> 80.6 us (0.22)
  waiting for transfers between devices: 281 us -> 0 us
  Pallas kernels: 0 us -> 76.5 us
  blocking collectives: 50.3 us -> 0 us
  local copies, waits for them, and re-layouts: 20.5 us -> 2.91 us
  between operations: 13.3 us -> 0.01 us
  matrix products: 8.08 us -> 0 us
    all_gather x3 -> x0, waiting for transfers between devices: 158 us -> none  [the longest x1 123 us: on_device(): every_tile = lax.all_gather(full_vectors, 'right', axis=0, tiled=True)]
    reduce_scatter x2 -> x0, waiting for transfers between devices: 122 us -> none  [the longest x1 92.8 us: on_device(): summed = lax.psum_scatter(placed, 'right', scatter_dimension=2, tiled=True)]
    pallas_call x0 -> x1, Pallas kernels: none -> 76.5 us  [on_device(): pl.pallas_call(kernel, out_shape=jax.ShapeDtypeStruct((4, 32, 128), f32),...]
    all_gather x2 -> x0, blocking collectives: 50.3 us -> none  [the longest x1 36.3 us: on_device(): amp_columns = lax.all_gather(amps, 'right', axis=3, tiled=True)]
    dot_general x2 -> x0, matrix products: 8.08 us -> none  [the longest x1 5.18 us: on_device(): jnp.einsum('xrq,tkq->txrk', left_rows, lax.all_gather(full_vectors, 'occ'...]
    dot_general x1 -> x0, local copies, waits for them, and re-layouts: 6.16 us -> none  [on_device(): jnp.einsum('trk,tkn->rn', swapped, lax.all_gather(own_amps, 'occ', axis=1...]
    transpose x1 -> x0, local copies, waits for them, and re-layouts: 5.93 us -> none  [on_device(): inner.reshape(tile_count, NTV, a_local, TV, TV, TV)]
  transfers between devices with their start and end apart: 5 -> 0, of which waited for: 5 -> 0; matrix products, arithmetic and copies ran while one was open for 6% -> 0% of each run, Pallas kernels for 0% -> 0%
where the time goes in v1:
time: 80.6 us; the launch traced here: 79.4 us
  Pallas kernels  76.5 us (95%)
  local copies, waits for them, and re-layouts  2.91 us (4%)
    pallas_call x1, Pallas kernels, on_device(): pl.pallas_call(kernel, out_shape=jax.ShapeDtypeStruct((4, 32, 128), f32),...  76.5 us

profile of v1, /device:TPU:1, one launch (start us, length us, event | category | flops | bytes accessed | tf_op | source)
XLA Modules:
  0.0 79.4 jit_solution(7383916994188776633)
XLA Ops:
  0.0 1.4 %reshape.3.listed = s32[256]{0:T(256)} reshape(s32[4,4,4,4]{3,2,1,0:T(4,128)} %param.5) | data formatting | bytes 2048 | tf_op jit(solution)/shard_map/reshape | solution.py:342
  1.4 76.5 %shard_map.37 = f32[4,32,128]{2,1,0:T(8,128)} custom-call(s32[256]{0:T(256)} %reshape.3.listed, bf16[128,512]{1,0:T(8,128)(2,1)} %bitcast.8, bf16[4,32,128]{2,1,0:T(8,128)(2,1)} %bitcast.9), custom_call_target="tpu_custom_call" | custom-call | tf_op jit(solution)/shard_map/pallas_call | solution.py:320
  77.9 1.5 %copy.5 = f32[1,4,128,32]{2,3,1,0:T(8,128)} copy(f32[1,4,128,32]{2,3,1,0:T(8,128)} %bitcast.7) | data formatting | bytes 131072

commit v2 on v1

v2 whole, which is shorter than its diff:
```python
import jax
import jax.numpy as jnp
from jax import lax
from jax.experimental import pallas as pl
from jax.experimental.pallas import tpu as pltpu
from jax.sharding import PartitionSpec as P

NTV = 4
MESH = pl.DeviceIdType.MESH
NT = (((1,), (1,)), ((), ()))


def kernel(
    chol, amps, listed, out,
    bd, xb, pb, tb, v, w, rs, rr, rx, ob, perm, live,
    bd_r, bdp_r, xb_r, pb_r, t1_r, t2_r, tx_r, tp_r, rr_r, ob_r, live_r,
    y_s, yf_s, z_s, x_s, bdp_s, pb_s, t1_s, t2_s, tx_s, tp_s, rr_s, ob_s,
):
    left = lax.axis_index("left")
    right = lax.axis_index("right")
    z = lax.axis_index("occ")
    yl, c = left // 2, left % 2
    x, yh = right // 4, right % 4
    y = 2 * yh + yl
    oc = 1 - c
    s = 1 - 2 * c
    xf, xk, xo = (x + s + 4) % 4, (x - s + 4) % 4, (x + 2) % 4
    zf, zk = (z + s + 8) % 8, (z - s + 8) % 8
    slot = y % 4
    ch = (1 + yl + yh % 2 + yh // 2) % 2
    own = (slot == 1) | (slot == 2)

    def dev(x_=x, y_=y, z_=z, c_=c):
        return (2 * (y_ % 2) + c_, 4 * x_ + y_ // 2, z_)

    def remote(src, dst, ssem, rsem, to):
        return pltpu.make_async_remote_copy(
            src_ref=src, dst_ref=dst, send_sem=ssem, recv_sem=rsem, device_id=to, device_id_type=MESH
        )

    def arrived(ref, sem):
        pltpu.make_async_copy(ref, ref, sem).wait()

    partner = dev(c_=oc)
    pair = dev(y_=y + 1 - 2 * yl)

    barrier = pltpu.get_barrier_semaphore()

    def greet(to):
        pl.semaphore_signal(barrier, inc=1, device_id=to, device_id_type=MESH)

    greet(partner)
    for k in range(1, 8):
        greet(dev(y_=(y + k) % 8))
        greet(dev(z_=(z + k) % 8))
    for k in range(1, 4):
        greet(dev(x_=(x + k) % 4))
    bd_own = pltpu.make_async_copy(chol, bd.at[yl, c, z], bd_r.at[yl, z])
    bd_own.start()
    pltpu.make_async_copy(listed, live, live_r).start()

    @pl.when(own)
    def _():
        pltpu.make_async_copy(chol, xb.at[x, slot], xb_r.at[x, slot]).start()

    t_rows = pl.ds(pl.multiple_of(yh * 32, 32), 32)
    @pl.when(ch == yl)
    def _():
        pltpu.make_async_copy(amps.at[yh], tb.at[c, x, z, t_rows], t1_r).start()

    spread = lax.broadcasted_iota(jnp.int32, (256, 256), 1)
    spread = (spread % 32) * 8 + spread // 32 == lax.broadcasted_iota(jnp.int32, (256, 256), 0)
    perm[...] = jnp.where(spread, 1.0, 0.0).astype(jnp.bfloat16)
    pl.semaphore_wait(barrier, 18)

    def t1(k):
        d = (yh + k) % 4
        to = dev(y_=2 * d + (1 + d % 2 + d // 2 + yl) % 2)
        return remote(amps.at[d], tb.at[c, x, z, t_rows], t1_s.at[k], t1_r, to)

    for k in (2, 1, 3):
        t1(k).start()

    @pl.when(ch != yl)
    def _():
        t1(0).start()

    to_pair = remote(chol, bd.at[yl, c, z], y_s.at[2], bd_r.at[yl, z], pair)

    @pl.when(own)
    def _():
        to_pair.start()

    up = y + 1 + (slot // 2) * (1 - slot % 2)
    down = y + 7 - (1 - slot // 2) * (slot % 2)
    near = [remote(chol, xb.at[x, slot], y_s.at[k], xb_r.at[x, slot], dev(y_=to % 8)) for k, to in enumerate((up, down))]
    near[0].start()
    near[1].start()

    def z_send(u, t, forward):
        yq = (yl + u) % 2
        zz = (z - s * t + 8) % 8 if forward else (z + s * t + 8) % 8
        src = chol if (u, t) == (0, 0) else bd.at[yq, c, zz]
        return remote(
            src, bd.at[yq, c, zz], z_s.at[0 if forward else 1, u, t], bd_r.at[yq, zz], dev(z_=zf if forward else zk)
        )

    def bd_wait(u, zz):
        yq = (yl + u) % 2
        arrived(bd.at[yq, c, zz], bd_r.at[yq, zz])

    def bd_share(u, zz):
        yq = (yl + u) % 2
        return remote(bd.at[yq, c, zz], bd.at[yq, c, zz], bdp_s.at[u, zz], bdp_r.at[yq, zz], partner)

    z_send(0, 0, True).start()
    z_send(0, 0, False).start()

    pow4 = (1 + 3 * (slot % 2)) * (1 + 15 * (slot // 2))
    hs4 = [
        sum(h * 4**i for i, h in enumerate(row)) // pow4 % 4
        for row in ((2, 1, 2, 1), (3, 0, 3, 0), (1, 2, 1, 2), (0, 3, 0, 3))
    ]

    def x_wait(a, h):
        arrived(xb.at[a, h], xb_r.at[a, h])

    def x_send(a, i, to, which):
        h = hs4[i]
        return remote(xb.at[a, h], xb.at[a, h], x_s.at[which, i], xb_r.at[a, h], dev(x_=to))

    def x_share(a, h):
        return remote(xb.at[a, h], pb.at[a // 2, h], pb_s.at[a // 2, h], pb_r.at[a // 2, h], partner)

    def x_share_if(a, h):
        @pl.when(a % 2 != c)
        def _():
            x_share(a, h).start()

    def y_pass(i, act):
        h = hs4[i]
        for to, go in ((y + slot, h < slot), (y + 5 + slot, h > slot)):
            @pl.when(own & go)
            def _(to=to):
                act(remote(xb.at[x, h], xb.at[x, h], yf_s.at[i], xb_r.at[x, h], dev(y_=to % 8)))

    def rows_in(i):
        h = hs4[i]
        x_wait(x, h)
        y_pass(i, lambda copy: copy.start())
        x_send(x, i, xf, 0).start()
        x_send(x, i, xk, 1).start()
        x_share_if(x, h)

    def t2(k):
        return remote(tb.at[c, x, z], tb.at[c, x, z], t2_s.at[k], t2_r.at[z], dev(z_=(z + k) % 8))

    def tx(a, to, which):
        return remote(tb.at[c, a], tb.at[c, a], tx_s.at[which], tx_r.at[a], dev(x_=to))

    def tx_wait(a):
        arrived(tb.at[c, a], tx_r.at[a])

    def t_share(a):
        return remote(tb.at[c, a], tb.at[c, a], tp_s.at[a], tp_r.at[a], partner)

    @pl.when(own)
    def _():
        rows_in(0)
        rows_in(1)
        pltpu.make_async_copy(xb.at[x, hs4[1]], bd.at[1 - yl, c, z], bd_r.at[1 - yl, z]).start()

    bd_wait(1, z)
    z_send(1, 0, True).start()
    z_send(1, 0, False).start()

    @pl.when(~own)
    def _():
        rows_in(0)

    bd_wait(0, z)
    bd_share(0, z).start()
    bd_share(1, z).start()

    arrived(tb.at[c, x, z], t1_r)
    for k in (1, 7, 2, 6, 3, 5, 4):
        t2(k).start()

    @pl.when(~own)
    def _():
        rows_in(1)

    def hop(i):
        h = hs4[i]
        x_wait(xk, h)
        x_send(xk, i, xf, 2).start()
        x_share_if(xk, h)
        x_wait(xf, h)
        x_share_if(xf, h)

    def hop2(i):
        h = hs4[i]
        x_wait(xo, h)
        x_share_if(xo, h)

    def zstep(j):
        u, t = j % 2, j // 2 + 1
        zz = (z - s * t + 8) % 8
        bd_wait(u, zz)
        if t < 4:
            z_send(u, t, True).start()
        bd_share(u, zz).start()
        if t < 4:
            zz = (z + s * t + 8) % 8
            bd_wait(u, zz)
            if t < 3:
                z_send(u, t, False).start()
            bd_share(u, zz).start()

    for j in range(6):
        zstep(j)
        if j < 2:
            rows_in(j + 2)
        if j < 4:
            hop(j)
        if j == 3:
            for k in range(1, 8):
                zk_ = (z + k) % 8
                arrived(tb.at[c, x, zk_], t2_r.at[zk_])
            tx(x, xf, 0).start()
            tx(x, xk, 1).start()
            t_share(x).start()
        if 2 <= j < 6:
            hop2(j - 2)

    arrived(live, live_r)
    scale = [
        [live[c + 2 * a, 2 * ch + cc, x, yh].astype(jnp.float32) for a in range(2)]
        for cc in range(2)
    ]
    group = lax.broadcasted_iota(jnp.int32, (8, 128), 1) // 32
    odd, high = group % 2 == 1, group >= 2

    def integrals(za, zb):
        for q in range(2):
            for zz in (za, zb):
                arrived(bd.at[q, oc, zz], bdp_r.at[q, zz])
        total = None
        for q in range(2):
            rows = [xb[c + 2 * a, 2 * cc + q] for cc in range(2) for a in range(2)]
            cols = jnp.concatenate([bd[q, c, za], bd[q, c, zb]], 0)
            part = lax.dot_general(jnp.concatenate(rows, 0), cols, NT, preferred_element_type=jnp.float32)
            total = part if total is None else total + part
            rows = [pb[a, 2 * cc + q] for cc in range(2) for a in range(2)]
            cols = jnp.concatenate([bd[q, oc, za], bd[q, oc, zb]], 0)
            total = total + lax.dot_general(
                jnp.concatenate(rows, 0), cols, NT, preferred_element_type=jnp.float32
            )
        for cc in range(2):
            lo = 256 * cc
            block = jnp.concatenate([total[lo + 128 * a : lo + 128 * a + 128] * scale[cc][a] for a in range(2)], 0)
            block = jnp.dot(perm[...], block.astype(jnp.bfloat16), preferred_element_type=jnp.float32)
            v[0, lo : lo + 256, :] = block[:, :128]
            v[1, lo : lo + 256, :] = block[:, 128:]

        def swap(i, carry):
            for k, zz in enumerate((za, zb)):
                r = [v[k, pl.ds(pl.multiple_of(i * 32 + 8 * j, 8), 8), :] for j in range(4)]
                p = [None] * 4
                for j in (0, 2):
                    p[j] = jnp.where(odd, pltpu.roll(r[j + 1], 32, 1), r[j])
                    p[j + 1] = jnp.where(odd, r[j + 1], pltpu.roll(r[j], 96, 1))
                b = [jnp.where(high, pltpu.roll(p[j + 2], 64, 1), p[j]) for j in (0, 1)]
                b += [jnp.where(high, p[j + 2], pltpu.roll(p[j], 64, 1)) for j in (0, 1)]
                w[i, pl.ds(pl.multiple_of(32 * zz, 32), 32), :] = jnp.concatenate(b, 0).astype(jnp.bfloat16)
            return carry

        lax.fori_loop(0, 16, swap, 0, unroll=8)

    for a in range(2):
        for h in range(4):
            arrived(pb.at[a, h], pb_r.at[a, h])

    def zi(k):
        return (z + s * k + 8) % 8

    zstep(6)
    integrals(z, zi(-1))
    tx_wait(xk)
    tx(xk, xf, 2).start()
    tx_wait(xf)
    t_share(xk).start()
    t_share(xf).start()
    integrals(zi(1), zi(-2))
    zstep(7)
    integrals(zi(2), zi(-3))
    integrals(zi(3), zi(-4))

    def contract(*ns):
        total = None
        for i in range(0, 16, 2):
            t = jnp.concatenate(
                [jnp.concatenate([tb[i // 8, n, i % 8], tb[i // 8, n, i % 8 + 1]], 1) for n in ns], 0
            )
            m = jnp.concatenate([w[i], w[i + 1]], 1)
            part = lax.dot_general(t, m, NT, preferred_element_type=jnp.float32)
            total = part if total is None else total + part
        total = jnp.dot(total.astype(jnp.bfloat16), perm[...], preferred_element_type=jnp.float32)
        total = total.astype(jnp.bfloat16)
        for j, n in enumerate(ns):
            for i in range(4):
                for a in range(2):
                    lo = 128 * j + 32 * i
                    rs[n, 2 * i + a] = total[lo : lo + 32, 128 * a : 128 * a + 128]

    far = (4, 3, 5, 2, 6, 1, 7)

    def r1(n, k):
        to = (y + k) % 8
        return remote(rs.at[n, to], rr.at[n, y], rr_s.at[n, k], rr_r.at[n], dev(y_=to))

    order = (x, xk, xf, xo)
    for ns in (order[:3], order[3:]):
        if len(ns) == 1:
            tx_wait(xo)
            t_share(xo).start()
        for n in ns:
            arrived(tb.at[oc, n], tp_r.at[n])
        contract(*ns)
        for n in ns:
            for k in far:
                r1(n, k).start()

    def r2(n):
        return remote(rx.at[n], ob.at[x], ob_s.at[n], ob_r.at[x], dev(x_=n))

    for i, n in enumerate(order):
        arrived(rr.at[n, pl.ds(0, 7)], rr_r.at[n])
        total = rs[n, y].astype(jnp.float32)
        for k in range(1, 8):
            total = total + rr[n, (y + k) % 8].astype(jnp.float32)
        if i == 0:
            out[x] = total
        else:
            rx[n] = total
            r2(n).start()

    near[0].wait_send()
    near[1].wait_send()

    @pl.when(own)
    def _():
        to_pair.wait_send()

    for k in range(1, 4):
        t1(k).wait_send()

    @pl.when(ch != yl)
    def _():
        t1(0).wait_send()

    for k in range(1, 8):
        t2(k).wait_send()
    for u in range(2):
        for t in range(4):
            z_send(u, t, True).wait_send()
            if t < 3:
                z_send(u, t, False).wait_send()
        for zz in range(8):
            bd_share(u, zz).wait_send()
    for i in range(4):
        y_pass(i, lambda copy: copy.wait_send())
        x_send(x, i, xf, 0).wait_send()
        x_send(x, i, xk, 1).wait_send()
        x_send(xk, i, xf, 2).wait_send()
        t_share(i).wait_send()
        for a in range(2):
            x_share(oc + 2 * a, i).wait_send()
        for k in range(1, 8):
            r1(i, k).wait_send()
    tx(x, xf, 0).wait_send()
    tx(x, xk, 1).wait_send()
    tx(xk, xf, 2).wait_send()
    for n in order[1:]:
        r2(n).wait_send()
    for n in order[1:]:
        arrived(ob.at[n], ob_r.at[n])
        out[n] = ob[n]


def on_device(chol, amps, listed):
    bf16, f32, dma = jnp.bfloat16, jnp.float32, pltpu.SemaphoreType.DMA
    anyspace = pl.BlockSpec(memory_space=pl.ANY)
    out = pl.pallas_call(
        kernel,
        out_shape=jax.ShapeDtypeStruct((4, 32, 128), f32),
        in_specs=[anyspace, anyspace, anyspace],
        out_specs=pl.BlockSpec(memory_space=pltpu.VMEM),
        scratch_shapes=[
            pltpu.VMEM((2, 2, 8, 128, 512), bf16),
            pltpu.VMEM((4, 4, 128, 512), bf16),
            pltpu.VMEM((2, 4, 128, 512), bf16),
            pltpu.VMEM((2, 4, 8, 128, 128), bf16),
            pltpu.VMEM((2, 512, 128), f32),
            pltpu.VMEM((16, 256, 128), bf16),
            pltpu.VMEM((4, 8, 32, 128), bf16),
            pltpu.VMEM((4, 8, 32, 128), bf16),
            pltpu.VMEM((4, 32, 128), f32),
            pltpu.VMEM((4, 32, 128), f32),
            pltpu.VMEM((256, 256), bf16),
            pltpu.SMEM((4, 4, 4, 4), jnp.int32),
            dma((2, 8)), dma((2, 8)), dma((4, 4)), dma((2, 4)), dma, dma((8,)), dma((4,)), dma((4,)), dma((4,)), dma((4,)), dma,
            dma((3,)), dma((4,)), dma((2, 2, 4)), dma((3, 4)), dma((2, 8)), dma((2, 4)), dma((4,)), dma((8,)), dma((3,)), dma((4,)),
            dma((4, 8)), dma((4,)),
        ],
        compiler_params=pltpu.CompilerParams(
            collective_id=0, has_side_effects=True, vmem_limit_bytes=60 * 1024 * 1024
        ),
    )(chol[0], jnp.swapaxes(amps[0], 1, 2), listed)
    return jnp.swapaxes(out, 1, 2)[None]


def solution(mesh):
    placed = (P("right", "occ", "left"), P("left", None, "occ", "right"), P())
    return jax.shard_map(
        on_device,
        mesh=mesh,
        in_specs=placed,
        out_specs=P("left", None, "occ", "right"),
        check_vma=False,
    )
```

time: 80.6 us -> 68 us (0.84)
  Pallas kernels: 76.5 us -> 65.3 us
  local copies, waits for them, and re-layouts: 2.91 us -> 1.47 us
    pallas_call x1, Pallas kernels: 76.5 us -> 65.3 us  [on_device(): pl.pallas_call(kernel, out_shape=jax.ShapeDtypeStruct((4, 32, 128), f32),...]
    reshape x1 -> x0, local copies, waits for them, and re-layouts: 1.43 us -> none  [on_device(): listed.reshape(-1)]
where the time goes in v2:
time: 68 us; the launch traced here: 66.8 us
  Pallas kernels  65.3 us (96%)
  local copies, waits for them, and re-layouts  1.47 us (2%)
    pallas_call x1, Pallas kernels, on_device(): pl.pallas_call(kernel, out_shape=jax.ShapeDtypeStruct((4, 32, 128), f32),...  65.3 us
    unnamed x1, local copies, waits for them, and re-layouts  1.47 us

profile of v2, /device:TPU:1, one launch (start us, length us, event | category | flops | bytes accessed | tf_op | source)
XLA Modules:
  0.0 66.8 jit_solution(5591060402135391613)
XLA Ops:
  0.0 65.3 %shard_map.37 = f32[4,32,128]{2,1,0:T(8,128)} custom-call(bf16[128,512]{1,0:T(8,128)(2,1)} %bitcast.8, bf16[4,32,128]{2,1,0:T(8,128)(2,1)} %bitcast.9, s32[4,4,4,4]{3,2,1,0:T(4,128)} %listed.1), custom_call_target="tpu_custom_call" | custom-call | tf_op jit(solution)/shard_map/pallas_call | solution.py:394
  65.3 1.5 %copy.5 = f32[1,4,128,32]{2,3,1,0:T(8,128)} copy(f32[1,4,128,32]{2,3,1,0:T(8,128)} %bitcast.7) | data formatting | bytes 131072

commit v3 on v2

--- a/solution.py
+++ b/solution.py
@@ -12,9 +12,9 @@
 
 def kernel(
     chol, amps, listed, out,
-    bd, xb, pb, tb, v, w, rs, rr, rx, ob, perm, live,
-    bd_r, bdp_r, xb_r, pb_r, t1_r, t2_r, tx_r, tp_r, rr_r, ob_r, live_r,
-    y_s, yf_s, z_s, x_s, bdp_s, pb_s, t1_s, t2_s, tx_s, tp_s, rr_s, ob_s,
+    bd, xb, pb, tb, v, w, rs, rr, perm, live,
+    bd_r, bdp_r, xb_r, pb_r, t1_r, t2_r, tx_r, tp_r, rr_r, live_r,
+    y_s, yf_s, z_s, x_s, bdp_s, pb_s, t1_s, t2_s, tx_s, tp_s, rr_s,
 ):
     left = lax.axis_index("left")
     right = lax.axis_index("right")
@@ -51,10 +51,9 @@
 
     greet(partner)
     for k in range(1, 8):
-        greet(dev(y_=(y + k) % 8))
         greet(dev(z_=(z + k) % 8))
-    for k in range(1, 4):
-        greet(dev(x_=(x + k) % 4))
+    for k in range(1, 32):
+        greet(dev(x_=(x + k // 8) % 4, y_=(y + k) % 8))
     bd_own = pltpu.make_async_copy(chol, bd.at[yl, c, z], bd_r.at[yl, z])
     bd_own.start()
     pltpu.make_async_copy(listed, live, live_r).start()
@@ -71,7 +70,7 @@
     spread = lax.broadcasted_iota(jnp.int32, (256, 256), 1)
     spread = (spread % 32) * 8 + spread // 32 == lax.broadcasted_iota(jnp.int32, (256, 256), 0)
     perm[...] = jnp.where(spread, 1.0, 0.0).astype(jnp.bfloat16)
-    pl.semaphore_wait(barrier, 18)
+    pl.semaphore_wait(barrier, 39)
 
     def t1(k):
         d = (yh + k) % 4
@@ -91,11 +90,27 @@
     def _():
         to_pair.start()
 
-    up = y + 1 + (slot // 2) * (1 - slot % 2)
-    down = y + 7 - (1 - slot // 2) * (slot % 2)
-    near = [remote(chol, xb.at[x, slot], y_s.at[k], xb_r.at[x, slot], dev(y_=to % 8)) for k, to in enumerate((up, down))]
-    near[0].start()
-    near[1].start()
+    def near(d):
+        return remote(chol, xb.at[x, slot], y_s.at[d % 2], xb_r.at[x, slot], dev(y_=(y + 8 + 1 - 2 * d) % 8))
+
+    away = 1 - 2 * yl
+
+    def relay():
+        to = dev(y_=(y - away + 8) % 8)
+        block = (slot + away + 4) % 4
+        return remote(bd.at[1 - yl, c, z], xb.at[x, block], y_s.at[2], xb_r.at[x, block], to)
+
+    def to_near(act):
+        @pl.when(own)
+        def _():
+            act(remote(chol, xb.at[x, slot], y_s.at[0], xb_r.at[x, slot], dev(y_=(y - away + 8) % 8)))
+
+        @pl.when(~own)
+        def _():
+            act(near(0))
+            act(near(1))
+
+    to_near(lambda copy: copy.start())
 
     def z_send(u, t, forward):
         yq = (yl + u) % 2
@@ -119,7 +134,7 @@
     pow4 = (1 + 3 * (slot % 2)) * (1 + 15 * (slot // 2))
     hs4 = [
         sum(h * 4**i for i, h in enumerate(row)) // pow4 % 4
-        for row in ((2, 1, 2, 1), (3, 0, 3, 0), (1, 2, 1, 2), (0, 3, 0, 3))
+        for row in ((3, 1, 2, 0), (2, 0, 3, 1), (1, 2, 1, 2), (0, 3, 0, 3))
     ]
 
     def x_wait(a, h):
@@ -163,32 +178,6 @@
 
     def t_share(a):
         return remote(tb.at[c, a], tb.at[c, a], tp_s.at[a], tp_r.at[a], partner)
-
-    @pl.when(own)
-    def _():
-        rows_in(0)
-        rows_in(1)
-        pltpu.make_async_copy(xb.at[x, hs4[1]], bd.at[1 - yl, c, z], bd_r.at[1 - yl, z]).start()
-
-    bd_wait(1, z)
-    z_send(1, 0, True).start()
-    z_send(1, 0, False).start()
-
-    @pl.when(~own)
-    def _():
-        rows_in(0)
-
-    bd_wait(0, z)
-    bd_share(0, z).start()
-    bd_share(1, z).start()
-
-    arrived(tb.at[c, x, z], t1_r)
-    for k in (1, 7, 2, 6, 3, 5, 4):
-        t2(k).start()
-
-    @pl.when(~own)
-    def _():
-        rows_in(1)
 
     def hop(i):
         h = hs4[i]
@@ -217,21 +206,80 @@
                 z_send(u, t, False).start()
             bd_share(u, zz).start()
 
-    for j in range(6):
-        zstep(j)
-        if j < 2:
-            rows_in(j + 2)
-        if j < 4:
-            hop(j)
-        if j == 3:
-            for k in range(1, 8):
-                zk_ = (z + k) % 8
-                arrived(tb.at[c, x, zk_], t2_r.at[zk_])
-            tx(x, xf, 0).start()
-            tx(x, xk, 1).start()
-            t_share(x).start()
-        if 2 <= j < 6:
-            hop2(j - 2)
+    def amps_out():
+        for k in range(1, 8):
+            zk_ = (z + k) % 8
+            arrived(tb.at[c, x, zk_], t2_r.at[zk_])
+        tx(x, xf, 0).start()
+        tx(x, xk, 1).start()
+        t_share(x).start()
+
+    def pair_out():
+        bd_wait(1, z)
+        z_send(1, 0, True).start()
+        z_send(1, 0, False).start()
+
+    def own_share():
+        bd_wait(0, z)
+        bd_share(0, z).start()
+        bd_share(1, z).start()
+
+    def amps_along():
+        arrived(tb.at[c, x, z], t1_r)
+        for k in (1, 7, 2, 6, 3, 5, 4):
+            t2(k).start()
+
+    @pl.when(own)
+    def _():
+        rows_in(0)
+        rows_in(1)
+        pltpu.make_async_copy(xb.at[x, hs4[1]], bd.at[1 - yl, c, z], bd_r.at[1 - yl, z]).start()
+        pair_out()
+        amps_along()
+        own_share()
+        zstep(0)
+        rows_in(2)
+        hop(0)
+        zstep(1)
+        rows_in(3)
+        hop(1)
+        zstep(2)
+        hop(2)
+        hop2(0)
+        zstep(3)
+        hop(3)
+        amps_out()
+        hop2(1)
+        zstep(4)
+        hop2(2)
+        zstep(5)
+        hop2(3)
+
+    @pl.when(~own)
+    def _():
+        pair_out()
+        relay().start()
+        rows_in(0)
+        own_share()
+        amps_along()
+        zstep(0)
+        rows_in(1)
+        zstep(1)
+        hop(0)
+        rows_in(2)
+        hop(1)
+        zstep(2)
+        rows_in(3)
+        hop2(0)
+        hop(2)
+        zstep(3)
+        hop2(1)
+        hop(3)
+        amps_out()
+        zstep(4)
+        hop2(2)
+        zstep(5)
+        hop2(3)
 
     arrived(live, live_r)
     scale = [
@@ -275,7 +323,7 @@
                 w[i, pl.ds(pl.multiple_of(32 * zz, 32), 32), :] = jnp.concatenate(b, 0).astype(jnp.bfloat16)
             return carry
 
-        lax.fori_loop(0, 16, swap, 0, unroll=8)
+        lax.fori_loop(0, 16, swap, 0, unroll=16)
 
     for a in range(2):
         for h in range(4):
@@ -285,16 +333,17 @@
         return (z + s * k + 8) % 8
 
     zstep(6)
-    integrals(z, zi(-1))
     tx_wait(xk)
     tx(xk, xf, 2).start()
+    t_share(xk).start()
     tx_wait(xf)
-    t_share(xk).start()
     t_share(xf).start()
-    integrals(zi(1), zi(-2))
     zstep(7)
-    integrals(zi(2), zi(-3))
-    integrals(zi(3), zi(-4))
+    def rest(k, carry):
+        integrals(zi(k), zi(-k - 1))
+        return carry
+
+    lax.fori_loop(0, 4, rest, 0)
 
     def contract(*ns):
         total = None
@@ -317,7 +366,7 @@
 
     def r1(n, k):
         to = (y + k) % 8
-        return remote(rs.at[n, to], rr.at[n, y], rr_s.at[n, k], rr_r.at[n], dev(y_=to))
+        return remote(rs.at[n, to], rr.at[x, y], rr_s.at[n, k], rr_r.at[x], dev(x_=n, y_=to))
 
     order = (x, xk, xf, xo)
     for ns in (order[:3], order[3:]):
@@ -328,29 +377,31 @@
             arrived(tb.at[oc, n], tp_r.at[n])
         contract(*ns)
         for n in ns:
-            for k in far:
+            for k in far if n is x else far + (0,):
                 r1(n, k).start()
 
-    def r2(n):
-        return remote(rx.at[n], ob.at[x], ob_s.at[n], ob_r.at[x], dev(x_=n))
-
-    for i, n in enumerate(order):
-        arrived(rr.at[n, pl.ds(0, 7)], rr_r.at[n])
-        total = rs[n, y].astype(jnp.float32)
+    def add_up(n):
+        total = rr[n, 0].astype(jnp.float32)
         for k in range(1, 8):
-            total = total + rr[n, (y + k) % 8].astype(jnp.float32)
-        if i == 0:
-            out[x] = total
-        else:
-            rx[n] = total
-            r2(n).start()
-
-    near[0].wait_send()
-    near[1].wait_send()
+            total = total + rr[n, k].astype(jnp.float32)
+        out[n] = total
+
+    arrived(rr.at[x, pl.ds(0, 7)], rr_r.at[x])
+    rr[x, y] = rs[x, y]
+    add_up(x)
+    for n in order[1:]:
+        arrived(rr.at[n], rr_r.at[n])
+        add_up(n)
+
+    to_near(lambda copy: copy.wait_send())
 
     @pl.when(own)
     def _():
         to_pair.wait_send()
+
+    @pl.when(~own)
+    def _():
+        relay().wait_send()
 
     for k in range(1, 4):
         t1(k).wait_send()
@@ -376,16 +427,12 @@
         t_share(i).wait_send()
         for a in range(2):
             x_share(oc + 2 * a, i).wait_send()
-        for k in range(1, 8):
-            r1(i, k).wait_send()
     tx(x, xf, 0).wait_send()
     tx(x, xk, 1).wait_send()
     tx(xk, xf, 2).wait_send()
-    for n in order[1:]:
-        r2(n).wait_send()
-    for n in order[1:]:
-        arrived(ob.at[n], ob_r.at[n])
-        out[n] = ob[n]
+    for n in order:
+        for k in far if n is x else far + (0,):
+            r1(n, k).wait_send()
 
 
 def on_device(chol, amps, listed):
@@ -405,13 +452,11 @@
             pltpu.VMEM((16, 256, 128), bf16),
             pltpu.VMEM((4, 8, 32, 128), bf16),
             pltpu.VMEM((4, 8, 32, 128), bf16),
-            pltpu.VMEM((4, 32, 128), f32),
-            pltpu.VMEM((4, 32, 128), f32),
             pltpu.VMEM((256, 256), bf16),
             pltpu.SMEM((4, 4, 4, 4), jnp.int32),
-            dma((2, 8)), dma((2, 8)), dma((4, 4)), dma((2, 4)), dma, dma((8,)), dma((4,)), dma((4,)), dma((4,)), dma((4,)), dma,
+            dma((2, 8)), dma((2, 8)), dma((4, 4)), dma((2, 4)), dma, dma((8,)), dma((4,)), dma((4,)), dma((4,)), dma,
             dma((3,)), dma((4,)), dma((2, 2, 4)), dma((3, 4)), dma((2, 8)), dma((2, 4)), dma((4,)), dma((8,)), dma((3,)), dma((4,)),
-            dma((4, 8)), dma((4,)),
+            dma((4, 8)),
         ],
         compiler_params=pltpu.CompilerParams(
             collective_id=0, has_side_effects=True, vmem_limit_bytes=60 * 1024 * 1024

time: 68 us -> 66.1 us (0.972); the launches traced: 66.8 us -> 66 us
  Pallas kernels: 65.3 us -> 64.5 us
    pallas_call x1, Pallas kernels: 65.3 us -> 64.5 us  [on_device(): pl.pallas_call(kernel, out_shape=jax.ShapeDtypeStruct((4, 32, 128), f32),...]
where the time goes in v3:
time: 66.1 us; the launch traced here: 66 us
  Pallas kernels  64.5 us (98%)
  local copies, waits for them, and re-layouts  1.47 us (2%)
    pallas_call x1, Pallas kernels, on_device(): pl.pallas_call(kernel, out_shape=jax.ShapeDtypeStruct((4, 32, 128), f32),...  64.5 us
    unnamed x1, local copies, waits for them, and re-layouts  1.47 us

profile of v3, /device:TPU:1, one launch (start us, length us, event | category | flops | bytes accessed | tf_op | source)
XLA Modules:
  0.0 66.0 jit_solution(2966606909321218295)
XLA Ops:
  0.0 64.5 %shard_map.37 = f32[4,32,128]{2,1,0:T(8,128)} custom-call(bf16[128,512]{1,0:T(8,128)(2,1)} %bitcast.8, bf16[4,32,128]{2,1,0:T(8,128)(2,1)} %bitcast.9, s32[4,4,4,4]{3,2,1,0:T(4,128)} %listed.1), custom_call_target="tpu_custom_call" | custom-call | tf_op jit(solution)/shard_map/pallas_call | solution.py:441
  64.5 1.5 %copy.5 = f32[1,4,128,32]{2,3,1,0:T(8,128)} copy(f32[1,4,128,32]{2,3,1,0:T(8,128)} %bitcast.7) | data formatting | bytes 131072

commit v4 on v3

--- a/solution.py
+++ b/solution.py
@@ -333,17 +333,22 @@
         return (z + s * k + 8) % 8
 
     zstep(6)
-    tx_wait(xk)
-    tx(xk, xf, 2).start()
-    t_share(xk).start()
-    tx_wait(xf)
-    t_share(xf).start()
-    zstep(7)
-    def rest(k, carry):
+
+    def piece(k, carry):
         integrals(zi(k), zi(-k - 1))
+
+        @pl.when(k == 0)
+        def _():
+            tx_wait(xk)
+            tx(xk, xf, 2).start()
+            t_share(xk).start()
+            tx_wait(xf)
+            t_share(xf).start()
+            zstep(7)
+
         return carry
 
-    lax.fori_loop(0, 4, rest, 0)
+    lax.fori_loop(0, 4, piece, 0)
 
     def contract(*ns):
         total = None

time: 66.1 us -> 65.8 us (level)
  no operation moved by 1% of the time
where the time goes in v4:
time: 65.8 us; the launch traced here: 65.7 us
  Pallas kernels  64.2 us (98%)
  local copies, waits for them, and re-layouts  1.47 us (2%)
    pallas_call x1, Pallas kernels, on_device(): pl.pallas_call(kernel, out_shape=jax.ShapeDtypeStruct((4, 32, 128), f32),...  64.2 us
    unnamed x1, local copies, waits for them, and re-layouts  1.47 us

profile of v4, /device:TPU:1, one launch (start us, length us, event | category | flops | bytes accessed | tf_op | source)
XLA Modules:
  0.0 65.7 jit_solution(9982029788213497585)
XLA Ops:
  0.0 64.2 %shard_map.37 = f32[4,32,128]{2,1,0:T(8,128)} custom-call(bf16[128,512]{1,0:T(8,128)(2,1)} %bitcast.8, bf16[4,32,128]{2,1,0:T(8,128)(2,1)} %bitcast.9, s32[4,4,4,4]{3,2,1,0:T(4,128)} %listed.1), custom_call_target="tpu_custom_call" | custom-call | tf_op jit(solution)/shard_map/pallas_call | solution.py:446
  64.2 1.5 %copy.5 = f32[1,4,128,32]{2,3,1,0:T(8,128)} copy(f32[1,4,128,32]{2,3,1,0:T(8,128)} %bitcast.7) | data formatting | bytes 131072
